TPU v7x, 256 devices: a whole 4x4x8 slice. The times are simulated.
256 devices in a mesh: grp: 16 (over z, core), ep: 16 (over y, x).
Axes of the slice: x: 4, y: 4, z: 8, core: 2. Of those that a mesh axis runs over, the one named last changes fastest.
Arguments:
- queries: bfloat16 [1024, 64, 576], P(('grp', 'ep')), may hold values from -75 to 75
- cache: bfloat16 [1024, 256, 576], P(('grp', 'ep')), may hold values from -6 to 6
- lengths: int32 [1024], P(('grp', 'ep')), may hold values from 2 to 256, as said below
- live_rows: int32 [256], P(('grp', 'ep')), may hold values from 1 to 4, as said below
- tokens: bfloat16 [4096, 3584], P(('grp', 'ep')), may hold values from -6 to 6
- ids: int32 [4096, 8], P(('grp', 'ep')), may hold values from 0 to 127, all different within a row; in each aligned block of 16 rows (0 to 15, 16 to 31, ...) at most 2 rows name the same one
- gates: float32 [4096, 8], P(('grp', 'ep')), may hold values from 0.1 to 1
- w_gate: bfloat16 [256, 3584, 512], P(('grp', 'ep')), may hold values from -0.09375 to 0.09375
- w_up: bfloat16 [256, 3584, 512], P(('grp', 'ep')), may hold values from -0.09375 to 0.09375
- w_down: bfloat16 [256, 512, 3584], P(('grp', 'ep')), may hold values from -0.1875 to 0.1875
Outputs:
- context: bfloat16 [1024, 64, 512], P(('grp', 'ep'))
- mixed: bfloat16 [4096, 3584], P(('grp', 'ep'))
Inputs may be any that keep to these rules, and one draw needn't show every extreme that they name: `ids`: each row names 8 different experts; among the rows of one device no expert is named more than 2 times. `lengths`: the first request slot of every device holds 256 positions. `live_rows`: a device's live request slots are its first ones; on a quarter of the grp indices every device holds 2 or fewer, elsewhere exactly 4.
All inputs are finite; a program needn't handle non-finite values.
Results may differ from a plain program's by a relative error of at most 0.012.
Values may be sent and summed in bfloat16 or wider, within the bound.
A program may use at most 128 MiB of HBM per device.

v0:
```python
import jax
import jax.numpy as jnp
from jax import lax
from jax.sharding import PartitionSpec as P

TOPK = 8
LAT = 512
CAP = 2
score_scale = 192.0 ** (-0.5)
neg_large = -1e30


def attend(queries, cache, lengths, live_count):
    scores = (
        jnp.einsum("rhc,rlc->rhl", queries, cache, preferred_element_type=jnp.float32) * score_scale
    )
    positions = lax.broadcasted_iota(jnp.int32, scores.shape, 2)
    inside = positions < lengths[:, None, None]
    masked = jnp.where(inside, scores, neg_large)
    highest = jnp.max(masked, axis=2, keepdims=True)
    powers = jnp.where(inside, jnp.exp(masked - highest), 0.0)
    totals = jnp.sum(powers, axis=2, keepdims=True)
    weights = (powers / totals).astype(jnp.bfloat16)
    context = jnp.einsum(
        "rhl,rlc->rhc", weights, cache[:, :, :LAT], preferred_element_type=jnp.float32
    ).astype(jnp.bfloat16)
    request_slot = lax.broadcasted_iota(jnp.int32, context.shape, 0)
    return jnp.where(request_slot < live_count, context, jnp.zeros_like(context))


def expert_partial(flat_rows, w_gate, w_up, w_down):
    gate_part = jnp.dot(flat_rows, w_gate[0], preferred_element_type=jnp.float32)
    up_part = jnp.dot(flat_rows, w_up[0], preferred_element_type=jnp.float32)
    hidden = (jax.nn.silu(gate_part) * up_part).astype(jnp.bfloat16)
    return jnp.dot(hidden, w_down[0], preferred_element_type=jnp.float32)


def per_device(queries, cache, lengths, live_rows, tokens, ids, gates, w_gate, w_up, w_down):
    context = attend(queries, cache, lengths, live_rows[0])
    group_count = lax.axis_size("grp")
    peer_count = lax.axis_size("ep")
    pair_count = peer_count // 2
    row_count = tokens.shape[0]
    feature = tokens.shape[1]
    expert_slots = group_count * CAP
    slot_count = pair_count * expert_slots
    column_rows = group_count * row_count
    all_tokens = lax.all_gather(tokens, "grp", axis=0, tiled=True)
    all_ids = lax.all_gather(ids, "grp", axis=0, tiled=True)
    all_gates = lax.all_gather(gates, "grp", axis=0, tiled=True)
    my_group = lax.axis_index("grp")
    local = all_ids - pair_count * my_group
    experts = jnp.arange(pair_count, dtype=jnp.int32)
    pick_hot = (local[:, :, None] == experts[None, None, :]).astype(jnp.int32)
    token_hot = jnp.sum(pick_hot, axis=1)
    gate_of = jnp.sum(all_gates[:, :, None] * pick_hot.astype(jnp.float32), axis=1)
    blocks = token_hot.reshape(group_count, row_count, pair_count)
    earlier = (jnp.cumsum(blocks, axis=1) - blocks).reshape(column_rows, pair_count)
    source = jnp.arange(column_rows, dtype=jnp.int32)[:, None] // row_count
    slot_id = experts[None, :] * expert_slots + source * CAP + earlier
    slot_id = jnp.where(token_hot > 0, slot_id, slot_count)
    slots = jnp.arange(slot_count, dtype=jnp.int32)
    match = slot_id[:, :, None] == slots[None, None, :]
    dispatch = jnp.any(match, axis=1).T.astype(jnp.bfloat16)
    combine = jnp.sum(jnp.where(match, gate_of[:, :, None], 0.0), axis=1)
    outgoing = jnp.dot(dispatch, all_tokens, preferred_element_type=jnp.float32).astype(
        jnp.bfloat16
    )
    doubled = jnp.repeat(outgoing.reshape(pair_count, expert_slots, feature), 2, axis=0)
    arriving = lax.all_to_all(doubled, "ep", split_axis=0, concat_axis=0, tiled=True)
    partials = expert_partial(
        arriving.reshape(peer_count * expert_slots, feature), w_gate, w_up, w_down
    ).astype(jnp.bfloat16)
    returned = lax.all_to_all(
        partials.reshape(peer_count, expert_slots, feature),
        "ep",
        split_axis=0,
        concat_axis=0,
        tiled=True,
    )
    expert_out = (
        returned.reshape(pair_count, 2, expert_slots, feature)
        .astype(jnp.float32)
        .sum(axis=1)
        .astype(jnp.bfloat16)
        .reshape(slot_count, feature)
    )
    column_mixed = jnp.dot(
        combine,
        expert_out.astype(jnp.float32),
        precision=lax.Precision.HIGHEST,
        preferred_element_type=jnp.float32,
    )
    mixed = lax.psum_scatter(column_mixed, "grp", scatter_dimension=0, tiled=True)
    return (context, mixed.astype(jnp.bfloat16))


def solution(mesh):
    in_specs = (
        P(("grp", "ep"), None, None),
        P(("grp", "ep"), None, None),
        P(("grp", "ep")),
        P(("grp", "ep")),
        P(("grp", "ep"), None),
        P(("grp", "ep"), None),
        P(("grp", "ep"), None),
        P(("grp", "ep"), None, None),
        P(("grp", "ep"), None, None),
        P(("grp", "ep"), None, None),
    )
    out_specs = (P(("grp", "ep"), None, None), P(("grp", "ep"), None))
    return jax.shard_map(
        per_device, mesh=mesh, in_specs=in_specs, out_specs=out_specs, check_vma=False
    )
```

profile of v0, /device:TPU:6, one launch (start us, length us, event | category | flops | bytes accessed | tf_op | source)
XLA Modules:
  0.0 251.7 jit_solution(4051258885842507781)
XLA Ops:
  7.2 0.7 all-gather.4.cloned.1.call-update
  7.9 20.4 %all-gather = s32[16,16,8]{1,2,0:T(8,128)S(1)} all-gather(s32[1,16,8]{1,2,0:T(8,128)} %bitcast.51), channel_id=1, replica_groups=mesh['grp'=16,'ep'=16] {'grp'}, dimensions={0}, use_global_device_ids=true | all-gather | bytes 8704 | tf_op jit(solution)/shard_map/all_gather | solution.py:49
  28.5 0.1 copy.31
  28.7 0.7 fusion.30
  29.6 0.1 copy.33
  29.8 0.7 fusion.6
  30.5 21.8 %all-gather.4.cloned.1.call-done = bf16[256,3584]{1,0:T(8,128)(2,1)} async-done(((bf16[16,3584]{1,0:T(8,128)(2,1)}), bf16[256,3584]{1,0:T(8,128)(2,1)}) %all-gather.4.cloned.1.call-update) | async-done | bytes 1835024 | tf_op jit(solution)/shard_map/all_gather | solution.py:48
  52.3 2.2 convolution_convert_fusion.1
  54.5 0.4 broadcast_in_dim.46
  54.9 50.4 %all_to_all.10 = bf16[16,32,3584]{2,1,0:T(8,128)(2,1)S(1)} all-to-all(bf16[16,32,3584]{2,1,0:T(8,128)(2,1)S(1)} %bitcast.45), channel_id=1, replica_groups=mesh['grp'=16,'ep'=16] {'ep'}, dimensions={0} | all-to-all | bytes 7340032 | tf_op jit(solution)/shard_map/all_to_all | solution.py:70
  105.3 1.8 copy-done.1
  107.1 2.0 fusion.4
  109.2 10.0 %convolution_convert_fusion = bf16[512,3584]{1,0:T(8,128)(2,1)} fusion(bf16[1,512,3584]{2,1,0:T(8,128)(2,1)} %param.19, bf16[512,3584]{1,0:T(8,128)(2,1)} %bitcast.50, bf16[1,3584,512]{2,1,0:T(8,128)(2,1)} %param.18, f32[512,512]{1,0:T(8,128)S(1)} %fusion.4), kind=kOutput, calls=%fused_computation.1 | convolution fusion | flops 3761504256 | bytes 15728640 | tf_op jit(solution)/shard_map/dot_general | solution.py:35
  119.2 7.1 %all-to-all-start.1 = ((bf16[16,32,3584]{2,1,0:T(8,128)(2,1)}), bf16[16,32,3584]{2,1,0:T(8,128)(2,1)}, u32[]{:S(2)}, u32[]{:S(2)}) async-start(bf16[16,32,3584]{2,1,0:T(8,128)(2,1)} %bitcast.48), calls=%async_computation.1 | async-start | bytes 7340032 | tf_op jit(solution)/shard_map/all_to_all | solution.py:74
  126.4 15.6 %all-gather.1 = f32[16,16,8]{1,2,0:T(8,128)S(1)} all-gather(f32[1,16,8]{1,2,0:T(8,128)S(1)} %bitcast.52), channel_id=1, replica_groups=mesh['grp'=16,'ep'=16] {'grp'}, dimensions={0}, use_global_device_ids=true | all-gather | bytes 8704 | tf_op jit(solution)/shard_map/all_gather | solution.py:50
  142.2 1.5 select_reduce_fusion
  143.7 33.3 %all-to-all-done.1 = bf16[16,32,3584]{2,1,0:T(8,128)(2,1)} async-done(((bf16[16,32,3584]{2,1,0:T(8,128)(2,1)}), bf16[16,32,3584]{2,1,0:T(8,128)(2,1)}, u32[]{:S(2)}, u32[]{:S(2)}) %all-to-all-start.1) | async-done | bytes 3670048 | tf_op jit(solution)/shard_map/all_to_all | solution.py:74
  176.9 2.8 %bitcast_reduce_fusion = bf16[8,32,3584]{2,1,0:T(8,128)(2,1)S(1)} fusion(bf16[16,32,3584]{2,1,0:T(8,128)(2,1)} %all-to-all-done.1), kind=kLoop, calls=%fused_computation.3 | loop fusion | flops 917504 | bytes 5505024 | tf_op jit(solution)/shard_map/reduce_sum | solution.py:84
  179.8 3.5 %fusion.31 = f32[256,3584]{1,0:T(8,128)} fusion(f32[256,256]{1,0:T(8,128)S(1)} %select_reduce_fusion, bf16[256,3584]{1,0:T(8,128)(2,1)S(1)} %bitcast.47), kind=kOutput, calls=%fused_computation.45 | convolution fusion | flops 2818572288 | bytes 5767168 | tf_op jit(solution)/shard_map/dot_general | solution.py:88
  183.9 0.3 fusion.14
  184.3 0.2 fusion.29
  184.5 1.2 fusion.17
  185.8 57.5 %reduce-scatter.2.cloned.1.call-done = f32[16,3584]{1,0:T(8,128)} async-done(((f32[256,3584]{1,0:T(8,128)}), f32[16,3584]{1,0:T(8,128)}) %reduce-scatter.2.cloned.1.call-update) | async-done | bytes 229392 | tf_op jit(solution)/shard_map/reduce_scatter | solution.py:94
  243.3 1.6 convert_element_type.35
  (29 shorter events, 0.9 us)
Async XLA Ops:
  7.2 176.8 %copy-start = (bf16[4,64,576]{2,1,0:T(8,128)(2,1)S(1)}, bf16[4,64,576]{2,1,0:T(8,128)(2,1)}, u32[]{:S(2)}) copy-start(bf16[4,64,576]{2,1,0:T(8,128)(2,1)} %param.10) | copy-start | bytes 884740
  7.2 45.1 %all-gather.4.cloned.1.call-start = ((), (), s32[]{:S(2)}) async-start(), calls=%async_computation.3 | async-start | bytes 1949696 | tf_op jit(solution)/shard_map/all_gather | solution.py:48
  54.9 52.2 %copy-start.5 = (bf16[1,3584,512]{2,1,0:T(8,128)(2,1)S(1)}, bf16[1,3584,512]{2,1,0:T(8,128)(2,1)}, u32[]{:S(2)}) copy-start(bf16[1,3584,512]{2,1,0:T(8,128)(2,1)} %param.17) | copy-start | bytes 11010052
  105.3 1.8 copy-start.1
  119.2 7.2 %copy-start.3 = (f32[16,8]{0,1:T(8,128)S(1)}, f32[16,8]{0,1:T(8,128)}, u32[]{:S(2)}) copy-start(f32[16,8]{0,1:T(8,128)} %param.16) | copy-start | bytes 1540
  119.2 57.7 %all-to-all-start.1 = ((bf16[16,32,3584]{2,1,0:T(8,128)(2,1)}), bf16[16,32,3584]{2,1,0:T(8,128)(2,1)}, u32[]{:S(2)}, u32[]{:S(2)}) async-start(bf16[16,32,3584]{2,1,0:T(8,128)(2,1)} %bitcast.48), calls=%async_computation.1 | async-start | bytes 7340032 | tf_op jit(solution)/shard_map/all_to_all | solution.py:74
  126.3 116.9 %reduce-scatter.2.cloned.1.call-start = ((), (), s32[]{:S(2)}) async-start(), calls=%async_computation.4 | async-start | bytes 3899392 | tf_op jit(solution)/shard_map/reduce_scatter | solution.py:94
  179.7 4.2 %copy-start.2 = (bf16[4,256,576]{1,2,0:T(8,128)(2,1)S(1)}, bf16[4,256,576]{1,2,0:T(8,128)(2,1)}, u32[]{:S(2)}) copy-start(bf16[4,256,576]{1,2,0:T(8,128)(2,1)} %param.11) | copy-start | bytes 3538948
  179.7 4.2 %copy-start.4 = (s32[4]{0:T(128)S(1)}, s32[4]{0:T(128)}, u32[]{:S(2)}) copy-start(s32[4]{0:T(128)} %param.12) | copy-start | bytes 52
Sparse Core Ops, SparseCore 0:
  9.8 42.4 all-gather.3
  183.4 59.8 reduce-scatter.1
where the time goes:
time: 252 us
  waiting for transfers between devices  113 us (45%)
  blocking collectives  86.3 us (34%)
  matrix products  19.4 us (8%)
  between operations  14.9 us (6%)
  other arithmetic  7.63 us (3%)
  starting transfers between devices  7.18 us (3%)
  local copies, waits for them, and re-layouts  3.1 us (1%)
    reduce_scatter x1, waiting for transfers between devices, per_device(): lax.psum_scatter(column_mixed, 'grp', scatter_dimension=0, tiled=True)  57.5 us
    all_to_all x1, blocking collectives, per_device(): lax.all_to_all(doubled, 'ep', split_axis=0, concat_axis=0, tiled=True)  50.4 us
    all_to_all x1, waiting for transfers between devices, per_device(): lax.all_to_all(partials.reshape(peer_count, expert_slots, feature), 'ep',...  33.3 us
    all_gather x1, waiting for transfers between devices, per_device(): all_tokens = lax.all_gather(tokens, 'grp', axis=0, tiled=True)  21.8 us
    all_gather x1, blocking collectives, per_device(): all_ids = lax.all_gather(ids, 'grp', axis=0, tiled=True)  20.4 us
    all_gather x1, blocking collectives, per_device(): all_gates = lax.all_gather(gates, 'grp', axis=0, tiled=True)  15.6 us
    dot_general x1, matrix products, expert_partial(): return jnp.dot(hidden, w_down[0], preferred_element_type=jnp.float32)  10 us
    all_to_all x1, starting transfers between devices, per_device(): lax.all_to_all(partials.reshape(peer_count, expert_slots, feature), 'ep',...  7.11 us
  transfers between devices with their start and end apart: 3, of which 3 were waited for; matrix products, arithmetic and copies ran while one was open for 2% of the time, Pallas kernels for 0%

commit v1 on v0

--- a/solution.py
+++ b/solution.py
@@ -46,7 +46,9 @@
     slot_count = pair_count * expert_slots
     column_rows = group_count * row_count
     all_tokens = lax.all_gather(tokens, "grp", axis=0, tiled=True)
-    all_ids = lax.all_gather(ids, "grp", axis=0, tiled=True)
+    all_ids = jnp.concatenate(
+        lax.all_to_all(jnp.stack([ids] * lax.axis_size("grp")), "grp", 0, 0), axis=0
+    )
     all_gates = lax.all_gather(gates, "grp", axis=0, tiled=True)
     my_group = lax.axis_index("grp")
     local = all_ids - pair_count * my_group

time: 252 us -> 252 us (level)
  blocking collectives: 86.3 us -> 66 us
  waiting for transfers between devices: 113 us -> 122 us
  starting transfers between devices: 7.18 us -> 15.7 us
    all_gather x1 -> x0, blocking collectives: 20.4 us -> none  [per_device(): all_ids = lax.all_gather(ids, 'grp', axis=0, tiled=True)]
    all_to_all x0 -> x1, starting transfers between devices: none -> 8.57 us  [per_device(): lax.all_to_all(jnp.stack([ids] * lax.axis_size('grp')), 'grp', 0, 0)]
    all_to_all x0 -> x1, waiting for transfers between devices: none -> 7.47 us  [per_device(): lax.all_to_all(jnp.stack([ids] * lax.axis_size('grp')), 'grp', 0, 0)]
  transfers between devices with their start and end apart: 3 -> 4, of which waited for: 3 -> 4; matrix products, arithmetic and copies ran while one was open for 2% -> 3% of each run, Pallas kernels for 0% -> 0%
where the time goes in v1:
time: 252 us
  waiting for transfers between devices  122 us (48%)
  blocking collectives  66 us (26%)
  matrix products  19.4 us (8%)
  starting transfers between devices  15.7 us (6%)
  between operations  14.9 us (6%)
  other arithmetic  8.3 us (3%)
  local copies, waits for them, and re-layouts  5.07 us (2%)
    reduce_scatter x1, waiting for transfers between devices, per_device(): lax.psum_scatter(column_mixed, 'grp', scatter_dimension=0, tiled=True)  57.5 us
    all_to_all x1, blocking collectives, per_device(): lax.all_to_all(doubled, 'ep', split_axis=0, concat_axis=0, tiled=True)  50.4 us
    all_to_all x1, waiting for transfers between devices, per_device(): lax.all_to_all(partials.reshape(peer_count, expert_slots, feature), 'ep',...  33.3 us
    all_gather x1, waiting for transfers between devices, per_device(): all_tokens = lax.all_gather(tokens, 'grp', axis=0, tiled=True)  23.4 us
    all_gather x1, blocking collectives, per_device(): all_gates = lax.all_gather(gates, 'grp', axis=0, tiled=True)  15.6 us
    dot_general x1, matrix products, expert_partial(): return jnp.dot(hidden, w_down[0], preferred_element_type=jnp.float32)  10.1 us
    all_to_all x1, starting transfers between devices, per_device(): lax.all_to_all(jnp.stack([ids] * lax.axis_size('grp')), 'grp', 0, 0)  8.57 us
    all_to_all x1, waiting for transfers between devices, per_device(): lax.all_to_all(jnp.stack([ids] * lax.axis_size('grp')), 'grp', 0, 0)  7.47 us
  transfers between devices with their start and end apart: 4, of which 4 were waited for; matrix products, arithmetic and copies ran while one was open for 3% of the time, Pallas kernels for 0%

profile of v1, /device:TPU:6, one launch (start us, length us, event | category | flops | bytes accessed | tf_op | source)
XLA Modules:
  0.0 251.8 jit_solution(9392191671633722607)
XLA Ops:
  7.2 0.7 all-gather.3.cloned.1.call-update
  7.9 0.7 broadcast_bitcast_fusion
  8.6 0.7 reshape.132
  9.3 8.6 %all-to-all-start = ((s32[16,1,128]{2,1,0:T(1,128)}), s32[16,1,128]{2,1,0:T(1,128)S(1)}, u32[]{:S(2)}, u32[]{:S(2)}) async-start(s32[16,1,128]{2,1,0:T(1,128)} %reshape.132), calls=%async_computation | async-start | bytes 16384 | tf_op jit(solution)/shard_map/all_to_all | solution.py:50
  17.9 7.5 %all-to-all-done = s32[16,1,128]{2,1,0:T(1,128)S(1)} async-done(((s32[16,1,128]{2,1,0:T(1,128)}), s32[16,1,128]{2,1,0:T(1,128)S(1)}, u32[]{:S(2)}, u32[]{:S(2)}) %all-to-all-start) | async-done | bytes 8224 | tf_op jit(solution)/shard_map/all_to_all | solution.py:50
  25.4 0.5 broadcast.94
  25.9 0.7 reduce.1
  27.0 0.7 fusion.30
  28.1 0.7 fusion.6
  28.8 23.4 %all-gather.3.cloned.1.call-done = bf16[256,3584]{1,0:T(8,128)(2,1)} async-done(((bf16[16,3584]{1,0:T(8,128)(2,1)}), bf16[256,3584]{1,0:T(8,128)(2,1)}) %all-gather.3.cloned.1.call-update) | async-done | bytes 1835024 | tf_op jit(solution)/shard_map/all_gather | solution.py:48
  52.3 2.2 convolution_convert_fusion.1
  54.9 50.4 %all_to_all.15 = bf16[16,32,3584]{2,1,0:T(8,128)(2,1)S(1)} all-to-all(bf16[16,32,3584]{2,1,0:T(8,128)(2,1)S(1)} %bitcast.48), channel_id=1, replica_groups=mesh['grp'=16,'ep'=16] {'ep'}, dimensions={0} | all-to-all | bytes 7340032 | tf_op jit(solution)/shard_map/all_to_all | solution.py:72
  105.3 1.8 copy-done.1
  107.1 2.1 fusion.4
  109.2 10.1 %convolution_convert_fusion = bf16[512,3584]{1,0:T(8,128)(2,1)} fusion(bf16[1,512,3584]{2,1,0:T(8,128)(2,1)} %param.19, bf16[512,3584]{1,0:T(8,128)(2,1)} %bitcast.53, bf16[1,3584,512]{2,1,0:T(8,128)(2,1)} %param.18, f32[512,512]{1,0:T(8,128)S(1)} %fusion.4), kind=kOutput, calls=%fused_computation.1 | convolution fusion | flops 3761504256 | bytes 15728640 | tf_op jit(solution)/shard_map/dot_general | solution.py:35
  119.2 7.1 %all-to-all-start.2 = ((bf16[16,32,3584]{2,1,0:T(8,128)(2,1)}), bf16[16,32,3584]{2,1,0:T(8,128)(2,1)}, u32[]{:S(2)}, u32[]{:S(2)}) async-start(bf16[16,32,3584]{2,1,0:T(8,128)(2,1)} %bitcast.51), calls=%async_computation.2 | async-start | bytes 7340032 | tf_op jit(solution)/shard_map/all_to_all | solution.py:76
  126.4 15.6 %all-gather = f32[16,16,8]{1,2,0:T(8,128)S(1)} all-gather(f32[1,16,8]{1,2,0:T(8,128)S(1)} %bitcast.54), channel_id=1, replica_groups=mesh['grp'=16,'ep'=16] {'grp'}, dimensions={0}, use_global_device_ids=true | all-gather | bytes 8704 | tf_op jit(solution)/shard_map/all_gather | solution.py:52
  142.2 1.5 select_reduce_fusion
  143.7 33.3 %all-to-all-done.2 = bf16[16,32,3584]{2,1,0:T(8,128)(2,1)} async-done(((bf16[16,32,3584]{2,1,0:T(8,128)(2,1)}), bf16[16,32,3584]{2,1,0:T(8,128)(2,1)}, u32[]{:S(2)}, u32[]{:S(2)}) %all-to-all-start.2) | async-done | bytes 3670048 | tf_op jit(solution)/shard_map/all_to_all | solution.py:76
  176.9 2.8 %bitcast_reduce_fusion = bf16[8,32,3584]{2,1,0:T(8,128)(2,1)S(1)} fusion(bf16[16,32,3584]{2,1,0:T(8,128)(2,1)} %all-to-all-done.2), kind=kLoop, calls=%fused_computation.3 | loop fusion | flops 917504 | bytes 5505024 | tf_op jit(solution)/shard_map/reduce_sum | solution.py:86
  179.7 3.5 %fusion.31 = f32[256,3584]{1,0:T(8,128)} fusion(f32[256,256]{1,0:T(8,128)S(1)} %select_reduce_fusion, bf16[256,3584]{1,0:T(8,128)(2,1)S(1)} %bitcast.50), kind=kOutput, calls=%fused_computation.46 | convolution fusion | flops 2818572288 | bytes 5767168 | tf_op jit(solution)/shard_map/dot_general | solution.py:90
  184.5 1.2 fusion.17
  185.8 57.5 %reduce-scatter.2.cloned.1.call-done = f32[16,3584]{1,0:T(8,128)} async-done(((f32[256,3584]{1,0:T(8,128)}), f32[16,3584]{1,0:T(8,128)}) %reduce-scatter.2.cloned.1.call-update) | async-done | bytes 229392 | tf_op jit(solution)/shard_map/reduce_scatter | solution.py:96
  243.3 1.6 convert_element_type.35
  (35 shorter events, 2.1 us)
Async XLA Ops:
  7.2 176.7 %copy-start = (bf16[4,64,576]{2,1,0:T(8,128)(2,1)S(1)}, bf16[4,64,576]{2,1,0:T(8,128)(2,1)}, u32[]{:S(2)}) copy-start(bf16[4,64,576]{2,1,0:T(8,128)(2,1)} %param.10) | copy-start | bytes 884740
  7.2 45.1 %all-gather.3.cloned.1.call-start = ((), (), s32[]{:S(2)}) async-start(), calls=%async_computation.4 | async-start | bytes 1949696 | tf_op jit(solution)/shard_map/all_gather | solution.py:48
  9.3 16.1 %all-to-all-start = ((s32[16,1,128]{2,1,0:T(1,128)}), s32[16,1,128]{2,1,0:T(1,128)S(1)}, u32[]{:S(2)}, u32[]{:S(2)}) async-start(s32[16,1,128]{2,1,0:T(1,128)} %reshape.132), calls=%async_computation | async-start | bytes 16384 | tf_op jit(solution)/shard_map/all_to_all | solution.py:50
  54.8 52.3 %copy-start.5 = (bf16[1,3584,512]{2,1,0:T(8,128)(2,1)S(1)}, bf16[1,3584,512]{2,1,0:T(8,128)(2,1)}, u32[]{:S(2)}) copy-start(bf16[1,3584,512]{2,1,0:T(8,128)(2,1)} %param.17) | copy-start | bytes 11010052
  105.3 1.8 copy-start.1
  119.2 7.2 %copy-start.3 = (f32[16,8]{0,1:T(8,128)S(1)}, f32[16,8]{0,1:T(8,128)}, u32[]{:S(2)}) copy-start(f32[16,8]{0,1:T(8,128)} %param.16) | copy-start | bytes 1540
  119.2 57.7 %all-to-all-start.2 = ((bf16[16,32,3584]{2,1,0:T(8,128)(2,1)}), bf16[16,32,3584]{2,1,0:T(8,128)(2,1)}, u32[]{:S(2)}, u32[]{:S(2)}) async-start(bf16[16,32,3584]{2,1,0:T(8,128)(2,1)} %bitcast.51), calls=%async_computation.2 | async-start | bytes 7340032 | tf_op jit(solution)/shard_map/all_to_all | solution.py:76
  126.3 117.0 %reduce-scatter.2.cloned.1.call-start = ((), (), s32[]{:S(2)}) async-start(), calls=%async_computation.5 | async-start | bytes 3899392 | tf_op jit(solution)/shard_map/reduce_scatter | solution.py:96
  179.7 4.2 %copy-start.2 = (bf16[4,256,576]{1,2,0:T(8,128)(2,1)S(1)}, bf16[4,256,576]{1,2,0:T(8,128)(2,1)}, u32[]{:S(2)}) copy-start(bf16[4,256,576]{1,2,0:T(8,128)(2,1)} %param.11) | copy-start | bytes 3538948
  179.7 4.2 %copy-start.4 = (s32[4]{0:T(128)S(1)}, s32[4]{0:T(128)}, u32[]{:S(2)}) copy-start(s32[4]{0:T(128)} %param.12) | copy-start | bytes 52
Sparse Core Ops, SparseCore 0:
  9.8 42.3 all-gather.2
  183.4 59.9 reduce-scatter.1
